TPU v7x, 32 devices: a whole 2x2x4 slice. The times are simulated.
32 devices in a mesh: groups: 2 (over y), tm: 16 (over z, x, core).
Axes of the slice: x: 2, y: 2, z: 4, core: 2. Of those that a mesh axis runs over, the one named last changes fastest.
Arguments:
- frames: bfloat16 [4096, 8192], P('tm', 'groups'), parts along dimension 1, may hold values from -6 to 6
- frame_valid: int32 [8192], P(('groups', 'tm')), parts along dimension 0, may hold values 0 or 1
- valid_count: int32 [32], P('groups'), parts along dimension 0, may hold values from 32 to 128, as said below
- block_map: int32 [32, 256], P('groups'), parts along dimension 0, may hold values from 0 to 255, as said below
- offsets: int32 [4, 2], replicated, may hold values from -4 to 4
Outputs:
- cross: float32 [512, 4, 2, 2048], P(('groups', 'tm')), parts along dimension 0
There are 2 independent parts, one for each index of `groups`. A program takes and returns all parts, laid end to end along the dimension named above; an argument that names none is the same for every part. Nothing has to cross between parts.
Inputs may be any that keep to these rules, and one draw needn't show every extreme that they name: `valid_count`: at most half of a tile's pixels are valid. Some tile has exactly 128 valid pixels and another exactly 32 in every draw; the others are spread evenly between the two. `block_map`: each row is a permutation of the pixels of a tile. Row steps lie in -4 to 4.
All inputs are finite; a program needn't handle non-finite values. No bound on the sum of `frame_valid` on one device may be relied on, other than what follows from the above.
Results may differ from a plain program's by a relative error of at most 0.0052.
Values may be sent and summed in bfloat16 or wider, within the bound.
No kernel may reach another device: no remote copies, remote signals or barrier semaphores. Data moves between devices by JAX's collectives and lax.ppermute only.
A program may use at most 64 MiB of HBM per device.

v0:
```python
import math
import jax
import jax.numpy as jnp
from jax import lax
from jax.sharding import PartitionSpec as P

ROWS = 16
BAND = 256
REACH = 4


def base_angles(frames_len, band_width):
    frame_idx = jnp.arange(frames_len, dtype=jnp.int32)[:, None]
    bin_idx = jnp.arange(band_width, dtype=jnp.int32)[None, :]
    angles = (frame_idx * bin_idx % frames_len).astype(jnp.float32) * (2.0 * math.pi / frames_len)
    return (jnp.cos(angles), jnp.sin(angles))


def rotated_table(base_cos, base_sin, bin_start):
    frames_len = base_cos.shape[0]
    frame_idx = jnp.arange(frames_len, dtype=jnp.int32)
    phase = (frame_idx * bin_start % frames_len).astype(jnp.float32) * (2.0 * math.pi / frames_len)
    phase_cos = jnp.cos(phase)[:, None]
    phase_sin = jnp.sin(phase)[:, None]
    scaling = 1.0 / math.sqrt(frames_len)
    real_part = base_cos * phase_cos - base_sin * phase_sin
    imag_part = -(base_sin * phase_cos + base_cos * phase_sin)
    return (jnp.concatenate([real_part, imag_part], axis=1) * scaling).astype(jnp.bfloat16)


def nearby_validity(valid_count, block_map, position):
    tile_pix = block_map.shape[1]
    padded_count = jnp.pad(valid_count, ((1, 1),))
    padded_map = jnp.pad(block_map, ((1, 1), (0, 0)))
    counts = lax.dynamic_slice_in_dim(padded_count, position, 3, 0)
    slots_map = lax.dynamic_slice_in_dim(padded_map, position, 3, 0)
    slot_idx = jnp.arange(tile_pix, dtype=jnp.int32)
    live = (slot_idx[None, :] < counts[:, None]).astype(jnp.float32)
    match = (slots_map[:, :, None] == slot_idx[None, None, :]).astype(jnp.float32)
    return jnp.sum(live[:, :, None] * match, axis=1)


def transform(columns, table):
    return lax.dot_general(
        columns, table, (((0,), (0,)), ((), ())), preferred_element_type=jnp.float32
    )


def cross_block(extended, ext_valid, offsets, tile_width):
    spectra = extended.astype(jnp.float32)
    row_count = spectra.shape[0]
    half = spectra.shape[2] // 2
    padded = jnp.pad(spectra, ((REACH, REACH), (0, 0), (0, 0)))
    padded_valid = jnp.pad(ext_valid, ((REACH, REACH), (0, 0)))
    own_spec = spectra[:, REACH : REACH + tile_width]
    own_valid = ext_valid[:, REACH : REACH + tile_width]
    own_real = own_spec[..., :half]
    own_imag = own_spec[..., half:]
    results = []
    for which in range(offsets.shape[0]):
        row_step = offsets[which, 0] + REACH
        col_step = offsets[which, 1] + REACH
        shifted = lax.dynamic_slice(
            padded, (row_step, col_step, jnp.int32(0)), (row_count, tile_width, 2 * half)
        )
        shifted_valid = lax.dynamic_slice(
            padded_valid, (row_step, col_step), (row_count, tile_width)
        )
        other_real = shifted[..., :half]
        other_imag = shifted[..., half:]
        real_part = jnp.sum(own_real * other_real + own_imag * other_imag, axis=0)
        imag_part = jnp.sum(own_imag * other_real - own_real * other_imag, axis=0)
        pair_count = jnp.sum(own_valid * shifted_valid, axis=0)
        scaling = 1.0 / jnp.maximum(pair_count, 1.0)
        results.append(jnp.stack([real_part, imag_part], axis=1) * scaling[:, None, None])
    return jnp.stack(results, axis=1)


def per_device(frames, frame_valid, valid_count, block_map, offsets):
    tile_count = lax.axis_size("tm")
    position = lax.axis_index("tm")
    frame_dev, pixel_count = frames.shape
    tile_pix = pixel_count // tile_count
    tile_width = tile_pix // ROWS
    masked = frames * frame_valid[:, None].astype(jnp.bfloat16)
    grouped = masked.reshape(frame_dev, tile_count, tile_pix)
    nearby = nearby_validity(valid_count, block_map, position).reshape(3, ROWS, tile_width)
    ext_valid = jnp.concatenate(
        [nearby[0][:, tile_width - REACH :], nearby[1], nearby[2][:, :REACH]], axis=1
    )
    own_valid = nearby[1].reshape(tile_pix)
    tiled = grouped.reshape(frame_dev, tile_count, ROWS, tile_width)
    blank = jnp.zeros((frame_dev, 1, ROWS, REACH), jnp.bfloat16)
    left_side = jnp.concatenate([blank, tiled[:, :-1, :, tile_width - REACH :]], axis=1)
    right_side = jnp.concatenate([tiled[:, 1:, :, :REACH], blank], axis=1)
    margins = jnp.concatenate([left_side, right_side], axis=3).reshape(
        frame_dev, tile_count, ROWS * 2 * REACH
    )
    tile_frames, margin_frames = (
        lax.all_to_all(grouped, "tm", split_axis=1, concat_axis=0, tiled=True),
        lax.all_to_all(margins, "tm", split_axis=1, concat_axis=0, tiled=True),
    )
    margin_frames = margin_frames.reshape(-1, ROWS * 2 * REACH)
    margin_valid = jnp.concatenate(
        [ext_valid[:, :REACH], ext_valid[:, REACH + tile_width :]], axis=1
    ).reshape(-1)
    tile_frames = tile_frames.reshape(-1, tile_pix)
    frames_len = tile_frames.shape[0]
    bins = frames_len // 2
    base_cos, base_sin = base_angles(frames_len, BAND)

    def own_spectra(table):
        spectra = transform(tile_frames, table) * own_valid[:, None]
        return spectra.astype(jnp.bfloat16).reshape(ROWS, tile_width, table.shape[1])

    def one_band(band_index, result):
        bin_start = (band_index * BAND).astype(jnp.int32)
        table = rotated_table(base_cos, base_sin, bin_start)
        own_spec = own_spectra(table)
        edge_spec = (transform(margin_frames, table) * margin_valid[:, None]).astype(jnp.bfloat16)
        edge_spec = edge_spec.reshape(ROWS, 2 * REACH, table.shape[1])
        extended = jnp.concatenate([edge_spec[:, :REACH], own_spec, edge_spec[:, REACH:]], axis=1)
        band_cross = cross_block(extended, ext_valid, offsets, tile_width)
        return lax.dynamic_update_slice(
            result, band_cross, (jnp.int32(0), jnp.int32(0), jnp.int32(0), bin_start)
        )

    result = jnp.zeros((tile_width, offsets.shape[0], 2, bins), jnp.float32)
    return lax.fori_loop(0, bins // BAND, one_band, result)


def solution(mesh):
    return jax.shard_map(
        per_device,
        mesh=mesh,
        in_specs=(P("tm", "groups"), P(("groups", "tm")), P("groups"), P("groups", None), P()),
        out_specs=P(("groups", "tm"), None, None, None),
        check_vma=False,
    )
```

profile of v0, /device:TPU:11, one launch (start us, length us, event | category | flops | bytes accessed | tf_op | source)
XLA Modules:
  0.0 280.0 jit_solution(15077811135383140968)
XLA Ops:
  0.0 3.3 %copy.13 = bf16[256,4096]{0,1:T(8,128)(2,1)S(1)} copy(bf16[256,4096]{1,0:T(8,128)(2,1)} %param.7) | data formatting | bytes 4194304 | tf_op args[0]
  3.3 1.5 broadcast_multiply_fusion
  4.8 2.0 fusion.44
  7.5 31.1 %all_to_all.30 = bf16[256,16,128]{0,2,1:T(8,128)(2,1)S(1)} all-to-all(bf16[256,16,128]{0,2,1:T(8,128)(2,1)S(1)} %fusion.41), channel_id=1, replica_groups=mesh['groups'=2,'tm'=16] {'tm'}, dimensions={1} | all-to-all | bytes 2097152 | tf_op jit(solution)/shard_map/all_to_all | solution.py:101
  38.6 4.9 %all-to-all-start.1 = ((bf16[256,16,256]{0,2,1:T(8,128)(2,1)}), bf16[256,16,256]{0,2,1:T(8,128)(2,1)S(1)}, u32[]{:S(2)}, u32[]{:S(2)}) async-start(bf16[256,16,256]{0,2,1:T(8,128)(2,1)} %bitcast.5), calls=%async_computation.1 | async-start | bytes 4194304 | tf_op jit(solution)/shard_map/all_to_all | solution.py:100
  55.4 1.3 copy.14
  56.7 34.2 %all-to-all-done.1 = bf16[256,16,256]{0,2,1:T(8,128)(2,1)S(1)} async-done(((bf16[256,16,256]{0,2,1:T(8,128)(2,1)}), bf16[256,16,256]{0,2,1:T(8,128)(2,1)S(1)}, u32[]{:S(2)}, u32[]{:S(2)}) %all-to-all-start.1) | async-done | bytes 2097184 | tf_op jit(solution)/shard_map/all_to_all | solution.py:100
  91.0 2.4 copy.15
  93.9 185.2 %while.19 = (s32[]{:T(128)}, f32[16,4,2,2048]{3,2,1,0:T(2,128)S(1)}, bf16[4096,128]{1,0:T(8,128)(2,1)}, f32[16,8]{1,0:T(8,128)}, bf16[4096,256]{1,0:T(8,128)(2,1...) while((s32[]{:T(128)}, ...), condition=%wide.wide.region_14.15_spmd.clone.clone, body=%wide.wide.region_1.14_spmd.clone.clone.sunk | while | flops 1649076224 | bytes 42145152 | solution.py:129
  94.1 17.5 %multiply_subtract_fusion.3 = (f32[4096,256]{1,0:T(8,128)S(1)}, f32[4096,256]{1,0:T(8,128)S(1)}) fusion(f32[4096]{0:T(1024)S(1)} %get-tuple-element.806, f32[4096]{0:T(1024)S(1)} %get-tuple-element.807), kind=kLoop, calls=%fused_computation.13.clone.clone.1 | loop fusion | flops 22020096 | bytes 8421376 | tf_op jit(solution)/shard_map/while/body/eval_jaxpr/sub | solution.py:26
  111.7 2.2 fusion.71
  117.3 17.5 %multiply_subtract_fusion.3 = (f32[4096,256]{1,0:T(8,128)S(1)}, f32[4096,256]{1,0:T(8,128)S(1)}) fusion(f32[4096]{0:T(1024)S(1)} %get-tuple-element.806, f32[4096]{0:T(1024)S(1)} %get-tuple-element.807), kind=kLoop, calls=%fused_computation.13.clone.clone.1 | loop fusion | flops 22020096 | bytes 8421376 | tf_op jit(solution)/shard_map/while/body/eval_jaxpr/sub | solution.py:26
  134.8 2.2 fusion.71
  137.1 1.3 fusion.73
  140.4 17.5 %multiply_subtract_fusion.3 = (f32[4096,256]{1,0:T(8,128)S(1)}, f32[4096,256]{1,0:T(8,128)S(1)}) fusion(f32[4096]{0:T(1024)S(1)} %get-tuple-element.806, f32[4096]{0:T(1024)S(1)} %get-tuple-element.807), kind=kLoop, calls=%fused_computation.13.clone.clone.1 | loop fusion | flops 22020096 | bytes 8421376 | tf_op jit(solution)/shard_map/while/body/eval_jaxpr/sub | solution.py:26
  157.9 2.2 fusion.71
  160.3 1.3 fusion.73
  163.5 17.5 %multiply_subtract_fusion.3 = (f32[4096,256]{1,0:T(8,128)S(1)}, f32[4096,256]{1,0:T(8,128)S(1)}) fusion(f32[4096]{0:T(1024)S(1)} %get-tuple-element.806, f32[4096]{0:T(1024)S(1)} %get-tuple-element.807), kind=kLoop, calls=%fused_computation.13.clone.clone.1 | loop fusion | flops 22020096 | bytes 8421376 | tf_op jit(solution)/shard_map/while/body/eval_jaxpr/sub | solution.py:26
  181.1 2.2 fusion.71
  183.4 1.3 fusion.73
  186.7 17.5 %multiply_subtract_fusion.3 = (f32[4096,256]{1,0:T(8,128)S(1)}, f32[4096,256]{1,0:T(8,128)S(1)}) fusion(f32[4096]{0:T(1024)S(1)} %get-tuple-element.806, f32[4096]{0:T(1024)S(1)} %get-tuple-element.807), kind=kLoop, calls=%fused_computation.13.clone.clone.1 | loop fusion | flops 22020096 | bytes 8421376 | tf_op jit(solution)/shard_map/while/body/eval_jaxpr/sub | solution.py:26
  204.2 2.2 fusion.71
  206.5 1.3 fusion.73
  209.8 17.5 %multiply_subtract_fusion.3 = (f32[4096,256]{1,0:T(8,128)S(1)}, f32[4096,256]{1,0:T(8,128)S(1)}) fusion(f32[4096]{0:T(1024)S(1)} %get-tuple-element.806, f32[4096]{0:T(1024)S(1)} %get-tuple-element.807), kind=kLoop, calls=%fused_computation.13.clone.clone.1 | loop fusion | flops 22020096 | bytes 8421376 | tf_op jit(solution)/shard_map/while/body/eval_jaxpr/sub | solution.py:26
  227.3 2.2 fusion.71
  229.6 1.3 fusion.73
  232.9 17.5 %multiply_subtract_fusion.3 = (f32[4096,256]{1,0:T(8,128)S(1)}, f32[4096,256]{1,0:T(8,128)S(1)}) fusion(f32[4096]{0:T(1024)S(1)} %get-tuple-element.806, f32[4096]{0:T(1024)S(1)} %get-tuple-element.807), kind=kLoop, calls=%fused_computation.13.clone.clone.1 | loop fusion | flops 22020096 | bytes 8421376 | tf_op jit(solution)/shard_map/while/body/eval_jaxpr/sub | solution.py:26
  250.5 2.2 fusion.71
  252.8 1.3 fusion.73
  256.0 17.5 %multiply_subtract_fusion.3 = (f32[4096,256]{1,0:T(8,128)S(1)}, f32[4096,256]{1,0:T(8,128)S(1)}) fusion(f32[4096]{0:T(1024)S(1)} %get-tuple-element.806, f32[4096]{0:T(1024)S(1)} %get-tuple-element.807), kind=kLoop, calls=%fused_computation.13.clone.clone.1 | loop fusion | flops 22020096 | bytes 8421376 | tf_op jit(solution)/shard_map/while/body/eval_jaxpr/sub | solution.py:26
  273.6 2.2 fusion.71
  275.9 1.3 fusion.73
  (217 shorter events, 20.4 us)
Async XLA Ops:
  0.0 3.3 %copy-start.6 = (s32[256]{0:T(256)S(1)}, s32[256]{0:T(256)}, u32[]{:S(2)}) copy-start(s32[256]{0:T(256)} %param.8) | copy-start | bytes 3076
  6.8 36.7 %copy-start.5 = (s32[4,2]{0,1:T(2,128)S(1)}, s32[4,2]{0,1:T(2,128)}, u32[]{:S(2)}) copy-start(s32[4,2]{0,1:T(2,128)} %param.11) | copy-start | bytes 100
  6.8 47.3 %copy-start.7 = (s32[16]{0:T(128)S(1)}, s32[16]{0:T(128)}, u32[]{:S(2)}) copy-start(s32[16]{0:T(128)} %param.9) | copy-start | bytes 196
  6.8 47.4 %copy-start.4 = (s32[16,256]{1,0:T(8,128)S(1)}, s32[16,256]{1,0:T(8,128)}, u32[]{:S(2)}) copy-start(s32[16,256]{1,0:T(8,128)} %param.10) | copy-start | bytes 49156
  38.6 52.3 %all-to-all-start.1 = ((bf16[256,16,256]{0,2,1:T(8,128)(2,1)}), bf16[256,16,256]{0,2,1:T(8,128)(2,1)S(1)}, u32[]{:S(2)}, u32[]{:S(2)}) async-start(bf16[256,16,256]{0,2,1:T(8,128)(2,1)} %bitcast.5), calls=%async_computation.1 | async-start | bytes 4194304 | tf_op jit(solution)/shard_map/all_to_all | solution.py:100
  55.0 38.8 %copy-start.2 = (f32[16,8]{1,0:T(8,128)}, f32[16,8]{1,0:T(8,128)S(1)}, u32[]{:S(2)}) copy-start(f32[16,8]{1,0:T(8,128)S(1)} %pad_maximum_fusion) | copy-start | bytes 1540
  55.3 38.6 %copy-start.3 = (f32[1,16,16]{2,1,0:T(8,128)}, f32[1,16,16]{2,1,0:T(8,128)S(1)}, u32[]{:S(2)}) copy-start(f32[1,16,16]{2,1,0:T(8,128)S(1)} %slice.243) | copy-start | bytes 3076
  111.7 2.3 copy-start
  134.8 2.3 copy-start
  157.9 2.3 copy-start
  181.1 2.3 copy-start
  204.2 2.3 copy-start
  227.3 2.3 copy-start
  250.4 2.3 copy-start
  273.6 2.3 copy-start
  279.1 1.0 copy-start.1
where the time goes:
time: 280 us
  other arithmetic  157 us (56%)
  waiting for transfers between devices  34.2 us (12%)
  blocking collectives  31.1 us (11%)
  matrix products  28.3 us (10%)
  local copies, waits for them, and re-layouts  13 us (5%)
  between operations  10.1 us (4%)
  starting transfers between devices  4.91 us (2%)
    sub x8, other arithmetic, rotated_table(): real_part = base_cos * phase_cos - base_sin * phase_sin  140 us
    all_to_all x1, waiting for transfers between devices, per_device(): lax.all_to_all(grouped, 'tm', split_axis=1, concat_axis=0, tiled=True)  34.2 us
    all_to_all x1, blocking collectives, per_device(): lax.all_to_all(margins, 'tm', split_axis=1, concat_axis=0, tiled=True)  31.1 us
    dot_general x16, matrix products, transform(): lax.dot_general(columns, table, (((0,), (0,)), ((), ())), preferred_eleme...  28.3 us
  transfers between devices with their start and end apart: 1, of which 1 were waited for; matrix products, arithmetic and copies ran while one was open for 1% of the time, Pallas kernels for 0%

commit v1 on v0

--- a/solution.py
+++ b/solution.py
@@ -7,6 +7,18 @@
 ROWS = 16
 BAND = 256
 REACH = 4
+
+
+def rotated_exchange(value, axis, split, join):
+    ways, here = (lax.axis_size(axis), lax.axis_index(axis))
+    width = value.shape[split] // ways
+    turned = jnp.roll(value, -here * width, axis=split)
+    got = [lax.slice_in_dim(turned, 0, width, axis=split)]
+    for far in range(1, ways):
+        sent = lax.slice_in_dim(turned, far * width, (far + 1) * width, axis=split)
+        got.append(lax.ppermute(sent, axis, [(d, (d + far) % ways) for d in range(ways)]))
+    line = jnp.concatenate(got[::-1], axis=join)
+    return jnp.roll(line, (here + 1) * got[0].shape[join], axis=join)
 
 
 def base_angles(frames_len, band_width):
@@ -98,7 +110,7 @@
     )
     tile_frames, margin_frames = (
         lax.all_to_all(grouped, "tm", split_axis=1, concat_axis=0, tiled=True),
-        lax.all_to_all(margins, "tm", split_axis=1, concat_axis=0, tiled=True),
+        rotated_exchange(margins, "tm", 1, 0),
     )
     margin_frames = margin_frames.reshape(-1, ROWS * 2 * REACH)
     margin_valid = jnp.concatenate(

time: 280 us -> 283 us (1.011); the launches traced: 280 us -> 278 us
  starting transfers between devices: 4.91 us -> 47.2 us
  blocking collectives: 31.1 us -> 0 us
  waiting for transfers between devices: 34.2 us -> 19.2 us
  matrix products: 28.3 us -> 17.6 us
  local copies, waits for them, and re-layouts: 13 us -> 19.5 us
  other arithmetic: 157 us -> 162 us
    ppermute x0 -> x15, starting transfers between devices: none -> 40 us  [rotated_exchange(): lax.ppermute(sent, axis, [(d, (d + far) % ways) for d in range(ways)])]
    all_to_all x1, waiting for transfers between devices: 34.2 us -> 0.01 us  [per_device(): lax.all_to_all(grouped, 'tm', split_axis=1, concat_axis=0, tiled=True)]
    all_to_all x1 -> x0, blocking collectives: 31.1 us -> none  [per_device(): lax.all_to_all(margins, 'tm', split_axis=1, concat_axis=0, tiled=True)]
    ppermute x0 -> x15, waiting for transfers between devices: none -> 19.1 us  [rotated_exchange(): lax.ppermute(sent, axis, [(d, (d + far) % ways) for d in range(ways)])]
    dot_general x16, matrix products: 28.3 us -> 17.6 us  [transform(): lax.dot_general(columns, table, (((0,), (0,)), ((), ())), preferred_eleme...]
    while x16 -> x32, local copies, waits for them, and re-layouts: 0.03 us -> 5.19 us
    dynamic_update_slice x8, other arithmetic: 0.7 us -> 5.76 us  [one_band(): lax.dynamic_update_slice(result, band_cross, (jnp.int32(0), jnp.int32(0),...]
  transfers between devices with their start and end apart: 1 -> 16, of which waited for: 1 -> 2; matrix products, arithmetic and copies ran while one was open for 1% -> 1% of each run, Pallas kernels for 0% -> 0%
where the time goes in v1:
time: 283 us; the launch traced here: 278 us
  other arithmetic  162 us (57%)
  starting transfers between devices  47.2 us (17%)
  local copies, waits for them, and re-layouts  19.5 us (7%)
  waiting for transfers between devices  19.2 us (7%)
  matrix products  17.6 us (6%)
  between operations  10.7 us (4%)
    sub x8, other arithmetic, rotated_table(): real_part = base_cos * phase_cos - base_sin * phase_sin  140 us
    ppermute x15, starting transfers between devices, rotated_exchange(): lax.ppermute(sent, axis, [(d, (d + far) % ways) for d in range(ways)])  40 us
    ppermute x15, waiting for transfers between devices, rotated_exchange(): lax.ppermute(sent, axis, [(d, (d + far) % ways) for d in range(ways)])  19.1 us
    dot_general x16, matrix products, transform(): lax.dot_general(columns, table, (((0,), (0,)), ((), ())), preferred_eleme...  17.6 us
    all_to_all x1, starting transfers between devices, per_device(): lax.all_to_all(grouped, 'tm', split_axis=1, concat_axis=0, tiled=True)  7.16 us
    dynamic_update_slice x8, other arithmetic, one_band(): lax.dynamic_update_slice(result, band_cross, (jnp.int32(0), jnp.int32(0),...  5.76 us
  transfers between devices with their start and end apart: 16, of which 2 were waited for; matrix products, arithmetic and copies ran while one was open for 1% of the time, Pallas kernels for 0%

profile of v1, /device:TPU:11, one launch (start us, length us, event | category | flops | bytes accessed | tf_op | source)
XLA Modules:
  0.0 277.5 jit_solution(4326087584479211529)
XLA Ops:
  0.0 3.3 %copy.13 = bf16[256,4096]{0,1:T(8,128)(2,1)S(1)} copy(bf16[256,4096]{1,0:T(8,128)(2,1)} %param.7) | data formatting | bytes 4194304 | tf_op args[0]
  3.3 1.5 broadcast_multiply_fusion
  4.8 2.0 fusion.45
  11.0 3.3 %collective-permute-start.3 = (bf16[256,1,128]{0,2,1:T(8,128)(2,1)}, bf16[256,1,128]{0,2,1:T(8,128)(2,1)S(1)}, u32[]{:S(2)}, u32[]{:S(2)}) collective-permute-start(bf16[256,1,128]{0,2,1:T(8,128)(2,1)} %get-tuple-element.592), channel_id=1, source_target_pairs={{0,12},{1,13},{2,14},{3,15},{4,0},{5,1},{6,2},{7,3},{8,4},{9,5},{1... | collective-permute-start | bytes 196616 | tf_op jit(solution)/shard_map/ppermute | solution.py:19
  14.5 7.2 %all-to-all-start = ((bf16[256,16,256]{0,2,1:T(8,128)(2,1)}), bf16[256,16,256]{0,2,1:T(8,128)(2,1)S(1)}, u32[]{:S(2)}, u32[]{:S(2)}) async-start(bf16[256,16,256]{0,2,1:T(8,128)(2,1)} %bitcast.3), calls=%async_computation | async-start | bytes 4194304 | tf_op jit(solution)/shard_map/all_to_all | solution.py:112
  34.0 3.8 %collective-permute-start.6 = (bf16[256,1,128]{0,2,1:T(8,128)(2,1)}, bf16[256,1,128]{0,2,1:T(8,128)(2,1)S(1)}, u32[]{:S(2)}, u32[]{:S(2)}) collective-permute-start(bf16[256,1,128]{0,2,1:T(8,128)(2,1)} %get-tuple-element.589), channel_id=1, source_target_pairs={{0,9},{1,10},{2,11},{3,12},{4,13},{5,14},{6,15},{7,0},{8,1},{9,2},... | collective-permute-start | bytes 196616 | tf_op jit(solution)/shard_map/ppermute | solution.py:19
  39.4 3.0 %collective-permute-start.9 = (bf16[256,1,128]{0,2,1:T(8,128)(2,1)}, bf16[256,1,128]{0,2,1:T(8,128)(2,1)S(1)}, u32[]{:S(2)}, u32[]{:S(2)}) collective-permute-start(bf16[256,1,128]{0,2,1:T(8,128)(2,1)} %get-tuple-element.586), channel_id=1, source_target_pairs={{0,6},{1,7},{2,8},{3,9},{4,10},{5,11},{6,12},{7,13},{8,14},{9,15},... | collective-permute-start | bytes 196616 | tf_op jit(solution)/shard_map/ppermute | solution.py:19
  42.5 17.4 %collective-permute-done.5 = bf16[256,1,128]{0,2,1:T(8,128)(2,1)S(1)} collective-permute-done((bf16[256,1,128]{0,2,1:T(8,128)(2,1)}, bf16[256,1,128]{0,2,1:T(8,128)(2,1)S(1)}, u32[]{:S(2)}, u32[]{:S(2)}) %collective-permute-start.5) | collective-permute-done | bytes 65568 | tf_op jit(solution)/shard_map/ppermute | solution.py:19
  59.8 3.0 %collective-permute-start.10 = (bf16[256,1,128]{0,2,1:T(8,128)(2,1)}, bf16[256,1,128]{0,2,1:T(8,128)(2,1)S(1)}, u32[]{:S(2)}, u32[]{:S(2)}) collective-permute-start(bf16[256,1,128]{0,2,1:T(8,128)(2,1)} %get-tuple-element.585), channel_id=1, source_target_pairs={{0,5},{1,6},{2,7},{3,8},{4,9},{5,10},{6,11},{7,12},{8,13},{9,14},{... | collective-permute-start | bytes 196616 | tf_op jit(solution)/shard_map/ppermute | solution.py:19
  62.9 13.0 %collective-permute-start.11 = (bf16[256,1,128]{0,2,1:T(8,128)(2,1)}, bf16[256,1,128]{0,2,1:T(8,128)(2,1)S(1)}, u32[]{:S(2)}, u32[]{:S(2)}) collective-permute-start(bf16[256,1,128]{0,2,1:T(8,128)(2,1)} %get-tuple-element.584), channel_id=1, source_target_pairs={{0,4},{1,5},{2,6},{3,7},{4,8},{5,9},{6,10},{7,11},{8,12},{9,13},{1... | collective-permute-start | bytes 196616 | tf_op jit(solution)/shard_map/ppermute | solution.py:19
  75.9 6.2 %collective-permute-start.12 = (bf16[256,1,128]{0,2,1:T(8,128)(2,1)}, bf16[256,1,128]{0,2,1:T(8,128)(2,1)S(1)}, u32[]{:S(2)}, u32[]{:S(2)}) collective-permute-start(bf16[256,1,128]{0,2,1:T(8,128)(2,1)} %get-tuple-element.583), channel_id=1, source_target_pairs={{0,3},{1,4},{2,5},{3,6},{4,7},{5,8},{6,9},{7,10},{8,11},{9,12},{10... | collective-permute-start | bytes 196616 | tf_op jit(solution)/shard_map/ppermute | solution.py:19
  82.1 1.8 collective-permute-start.13
  84.0 1.8 collective-permute-start.14
  85.9 1.7 collective-permute-done.14
  87.9 1.3 copy.14
  89.3 2.4 copy.15
  91.6 1.5 broadcast_in_dim.14
  93.1 184.4 %while.19 = (s32[]{:T(128)}, f32[16,4,2,2048]{3,2,1,0:T(2,128)}, bf16[4096,128]{1,0:T(8,128)(2,1)}, f32[16,8]{1,0:T(8,128)}, bf16[4096,256]{1,0:T(8,128)(2,1)}, ...) while((s32[]{:T(128)}, f32[16,4,2,2048]{3,2,1,0:T(2,128)}, ...), condition=%wide.wide.region_14.15_spmd.clone.clone, body=%wide.wide.region_1.14_spmd.clone.clone.sunk | while | flops 1649076224 | bytes 46339488 | solution.py:141
  93.2 17.5 %multiply_subtract_fusion.3 = (f32[4096,256]{1,0:T(8,128)S(1)}, f32[4096,256]{1,0:T(8,128)S(1)}) fusion(f32[4096]{0:T(1024)S(1)} %get-tuple-element.821, f32[4096]{0:T(1024)S(1)} %get-tuple-element.822), kind=kLoop, calls=%fused_computation.13.clone.clone.1 | loop fusion | flops 22020096 | bytes 8421376 | tf_op jit(solution)/shard_map/while/body/eval_jaxpr/sub | solution.py:38
  116.3 17.5 %multiply_subtract_fusion.3 = (f32[4096,256]{1,0:T(8,128)S(1)}, f32[4096,256]{1,0:T(8,128)S(1)}) fusion(f32[4096]{0:T(1024)S(1)} %get-tuple-element.821, f32[4096]{0:T(1024)S(1)} %get-tuple-element.822), kind=kLoop, calls=%fused_computation.13.clone.clone.1 | loop fusion | flops 22020096 | bytes 8421376 | tf_op jit(solution)/shard_map/while/body/eval_jaxpr/sub | solution.py:38
  135.4 1.3 fusion.75
  139.3 17.5 %multiply_subtract_fusion.3 = (f32[4096,256]{1,0:T(8,128)S(1)}, f32[4096,256]{1,0:T(8,128)S(1)}) fusion(f32[4096]{0:T(1024)S(1)} %get-tuple-element.821, f32[4096]{0:T(1024)S(1)} %get-tuple-element.822), kind=kLoop, calls=%fused_computation.13.clone.clone.1 | loop fusion | flops 22020096 | bytes 8421376 | tf_op jit(solution)/shard_map/while/body/eval_jaxpr/sub | solution.py:38
  158.5 1.3 fusion.75
  162.4 17.5 %multiply_subtract_fusion.3 = (f32[4096,256]{1,0:T(8,128)S(1)}, f32[4096,256]{1,0:T(8,128)S(1)}) fusion(f32[4096]{0:T(1024)S(1)} %get-tuple-element.821, f32[4096]{0:T(1024)S(1)} %get-tuple-element.822), kind=kLoop, calls=%fused_computation.13.clone.clone.1 | loop fusion | flops 22020096 | bytes 8421376 | tf_op jit(solution)/shard_map/while/body/eval_jaxpr/sub | solution.py:38
  181.5 1.3 fusion.75
  185.4 17.5 %multiply_subtract_fusion.3 = (f32[4096,256]{1,0:T(8,128)S(1)}, f32[4096,256]{1,0:T(8,128)S(1)}) fusion(f32[4096]{0:T(1024)S(1)} %get-tuple-element.821, f32[4096]{0:T(1024)S(1)} %get-tuple-element.822), kind=kLoop, calls=%fused_computation.13.clone.clone.1 | loop fusion | flops 22020096 | bytes 8421376 | tf_op jit(solution)/shard_map/while/body/eval_jaxpr/sub | solution.py:38
  208.5 17.5 %multiply_subtract_fusion.3 = (f32[4096,256]{1,0:T(8,128)S(1)}, f32[4096,256]{1,0:T(8,128)S(1)}) fusion(f32[4096]{0:T(1024)S(1)} %get-tuple-element.821, f32[4096]{0:T(1024)S(1)} %get-tuple-element.822), kind=kLoop, calls=%fused_computation.13.clone.clone.1 | loop fusion | flops 22020096 | bytes 8421376 | tf_op jit(solution)/shard_map/while/body/eval_jaxpr/sub | solution.py:38
  227.6 1.3 fusion.75
  231.5 17.5 %multiply_subtract_fusion.3 = (f32[4096,256]{1,0:T(8,128)S(1)}, f32[4096,256]{1,0:T(8,128)S(1)}) fusion(f32[4096]{0:T(1024)S(1)} %get-tuple-element.821, f32[4096]{0:T(1024)S(1)} %get-tuple-element.822), kind=kLoop, calls=%fused_computation.13.clone.clone.1 | loop fusion | flops 22020096 | bytes 8421376 | tf_op jit(solution)/shard_map/while/body/eval_jaxpr/sub | solution.py:38
  250.6 1.3 fusion.75
  254.6 17.5 %multiply_subtract_fusion.3 = (f32[4096,256]{1,0:T(8,128)S(1)}, f32[4096,256]{1,0:T(8,128)S(1)}) fusion(f32[4096]{0:T(1024)S(1)} %get-tuple-element.821, f32[4096]{0:T(1024)S(1)} %get-tuple-element.822), kind=kLoop, calls=%fused_computation.13.clone.clone.1 | loop fusion | flops 22020096 | bytes 8421376 | tf_op jit(solution)/shard_map/while/body/eval_jaxpr/sub | solution.py:38
  273.7 1.3 fusion.75
  (295 shorter events, 43.2 us)
Async XLA Ops:
  0.0 3.3 %copy-start.6 = (s32[256]{0:T(256)S(1)}, s32[256]{0:T(256)}, u32[]{:S(2)}) copy-start(s32[256]{0:T(256)} %param.8) | copy-start | bytes 3076
  8.8 25.1 %collective-permute-start = (bf16[256,1,128]{0,2,1:T(8,128)(2,1)}, bf16[256,1,128]{0,2,1:T(8,128)(2,1)S(1)}, u32[]{:S(2)}, u32[]{:S(2)}) collective-permute-start(bf16[256,1,128]{0,2,1:T(8,128)(2,1)} %get-tuple-element.595), channel_id=1, source_target_pairs={{0,15},{1,0},{2,1},{3,2},{4,3},{5,4},{6,5},{7,6},{8,7},{9,8},{10,9... | collective-permute-start | bytes 196616 | tf_op jit(solution)/shard_map/ppermute | solution.py:19
  9.5 24.6 %collective-permute-start.1 = (bf16[256,1,128]{0,2,1:T(8,128)(2,1)}, bf16[256,1,128]{0,2,1:T(8,128)(2,1)S(1)}, u32[]{:S(2)}, u32[]{:S(2)}) collective-permute-start(bf16[256,1,128]{0,2,1:T(8,128)(2,1)} %get-tuple-element.594), channel_id=1, source_target_pairs={{0,14},{1,15},{2,0},{3,1},{4,2},{5,3},{6,4},{7,5},{8,6},{9,7},{10,... | collective-permute-start | bytes 196616 | tf_op jit(solution)/shard_map/ppermute | solution.py:19
  9.7 28.1 %collective-permute-start.2 = (bf16[256,1,128]{0,2,1:T(8,128)(2,1)}, bf16[256,1,128]{0,2,1:T(8,128)(2,1)S(1)}, u32[]{:S(2)}, u32[]{:S(2)}) collective-permute-start(bf16[256,1,128]{0,2,1:T(8,128)(2,1)} %get-tuple-element.593), channel_id=1, source_target_pairs={{0,13},{1,14},{2,15},{3,0},{4,1},{5,2},{6,3},{7,4},{8,5},{9,6},{10... | collective-permute-start | bytes 196616 | tf_op jit(solution)/shard_map/ppermute | solution.py:19
  11.0 27.1 %collective-permute-start.3 = (bf16[256,1,128]{0,2,1:T(8,128)(2,1)}, bf16[256,1,128]{0,2,1:T(8,128)(2,1)S(1)}, u32[]{:S(2)}, u32[]{:S(2)}) collective-permute-start(bf16[256,1,128]{0,2,1:T(8,128)(2,1)} %get-tuple-element.592), channel_id=1, source_target_pairs={{0,12},{1,13},{2,14},{3,15},{4,0},{5,1},{6,2},{7,3},{8,4},{9,5},{1... | collective-permute-start | bytes 196616 | tf_op jit(solution)/shard_map/ppermute | solution.py:19
  14.3 25.1 %collective-permute-start.4 = (bf16[256,1,128]{0,2,1:T(8,128)(2,1)}, bf16[256,1,128]{0,2,1:T(8,128)(2,1)S(1)}, u32[]{:S(2)}, u32[]{:S(2)}) collective-permute-start(bf16[256,1,128]{0,2,1:T(8,128)(2,1)} %get-tuple-element.591), channel_id=1, source_target_pairs={{0,11},{1,12},{2,13},{3,14},{4,15},{5,0},{6,1},{7,2},{8,3},{9,4},{... | collective-permute-start | bytes 196616 | tf_op jit(solution)/shard_map/ppermute | solution.py:19
  14.5 7.2 %copy-start.5 = (s32[4,2]{0,1:T(2,128)S(1)}, s32[4,2]{0,1:T(2,128)}, u32[]{:S(2)}) copy-start(s32[4,2]{0,1:T(2,128)} %param.11) | copy-start | bytes 100
  14.5 18.2 %copy-start.7 = (s32[16]{0:T(128)S(1)}, s32[16]{0:T(128)}, u32[]{:S(2)}) copy-start(s32[16]{0:T(128)} %param.9) | copy-start | bytes 196
  14.5 18.3 %copy-start.4 = (s32[16,256]{1,0:T(8,128)S(1)}, s32[16,256]{1,0:T(8,128)}, u32[]{:S(2)}) copy-start(s32[16,256]{1,0:T(8,128)} %param.10) | copy-start | bytes 49156
  14.5 74.8 %all-to-all-start = ((bf16[256,16,256]{0,2,1:T(8,128)(2,1)}), bf16[256,16,256]{0,2,1:T(8,128)(2,1)S(1)}, u32[]{:S(2)}, u32[]{:S(2)}) async-start(bf16[256,16,256]{0,2,1:T(8,128)(2,1)} %bitcast.3), calls=%async_computation | async-start | bytes 4194304 | tf_op jit(solution)/shard_map/all_to_all | solution.py:112
  33.5 54.3 %copy-start.2 = (f32[16,8]{1,0:T(8,128)}, f32[16,8]{1,0:T(8,128)S(1)}, u32[]{:S(2)}) copy-start(f32[16,8]{1,0:T(8,128)S(1)} %pad_maximum_fusion) | copy-start | bytes 1540
  33.7 54.1 %copy-start.3 = (f32[1,16,16]{2,1,0:T(8,128)}, f32[1,16,16]{2,1,0:T(8,128)S(1)}, u32[]{:S(2)}) copy-start(f32[1,16,16]{2,1,0:T(8,128)S(1)} %slice.307) | copy-start | bytes 3076
  33.9 25.9 %collective-permute-start.5 = (bf16[256,1,128]{0,2,1:T(8,128)(2,1)}, bf16[256,1,128]{0,2,1:T(8,128)(2,1)S(1)}, u32[]{:S(2)}, u32[]{:S(2)}) collective-permute-start(bf16[256,1,128]{0,2,1:T(8,128)(2,1)} %get-tuple-element.590), channel_id=1, source_target_pairs={{0,10},{1,11},{2,12},{3,13},{4,14},{5,15},{6,0},{7,1},{8,2},{9,3},... | collective-permute-start | bytes 196616 | tf_op jit(solution)/shard_map/ppermute | solution.py:19
  34.0 28.8 %collective-permute-start.6 = (bf16[256,1,128]{0,2,1:T(8,128)(2,1)}, bf16[256,1,128]{0,2,1:T(8,128)(2,1)S(1)}, u32[]{:S(2)}, u32[]{:S(2)}) collective-permute-start(bf16[256,1,128]{0,2,1:T(8,128)(2,1)} %get-tuple-element.589), channel_id=1, source_target_pairs={{0,9},{1,10},{2,11},{3,12},{4,13},{5,14},{6,15},{7,0},{8,1},{9,2},... | collective-permute-start | bytes 196616 | tf_op jit(solution)/shard_map/ppermute | solution.py:19
  37.8 38.1 %collective-permute-start.7 = (bf16[256,1,128]{0,2,1:T(8,128)(2,1)}, bf16[256,1,128]{0,2,1:T(8,128)(2,1)S(1)}, u32[]{:S(2)}, u32[]{:S(2)}) collective-permute-start(bf16[256,1,128]{0,2,1:T(8,128)(2,1)} %get-tuple-element.588), channel_id=1, source_target_pairs={{0,8},{1,9},{2,10},{3,11},{4,12},{5,13},{6,14},{7,15},{8,0},{9,1},... | collective-permute-start | bytes 196616 | tf_op jit(solution)/shard_map/ppermute | solution.py:19
  38.2 43.9 %collective-permute-start.8 = (bf16[256,1,128]{0,2,1:T(8,128)(2,1)}, bf16[256,1,128]{0,2,1:T(8,128)(2,1)S(1)}, u32[]{:S(2)}, u32[]{:S(2)}) collective-permute-start(bf16[256,1,128]{0,2,1:T(8,128)(2,1)} %get-tuple-element.587), channel_id=1, source_target_pairs={{0,7},{1,8},{2,9},{3,10},{4,11},{5,12},{6,13},{7,14},{8,15},{9,0},... | collective-permute-start | bytes 196616 | tf_op jit(solution)/shard_map/ppermute | solution.py:19
  39.4 44.5 %collective-permute-start.9 = (bf16[256,1,128]{0,2,1:T(8,128)(2,1)}, bf16[256,1,128]{0,2,1:T(8,128)(2,1)S(1)}, u32[]{:S(2)}, u32[]{:S(2)}) collective-permute-start(bf16[256,1,128]{0,2,1:T(8,128)(2,1)} %get-tuple-element.586), channel_id=1, source_target_pairs={{0,6},{1,7},{2,8},{3,9},{4,10},{5,11},{6,12},{7,13},{8,14},{9,15},... | collective-permute-start | bytes 196616 | tf_op jit(solution)/shard_map/ppermute | solution.py:19
  59.8 25.9 %collective-permute-start.10 = (bf16[256,1,128]{0,2,1:T(8,128)(2,1)}, bf16[256,1,128]{0,2,1:T(8,128)(2,1)S(1)}, u32[]{:S(2)}, u32[]{:S(2)}) collective-permute-start(bf16[256,1,128]{0,2,1:T(8,128)(2,1)} %get-tuple-element.585), channel_id=1, source_target_pairs={{0,5},{1,6},{2,7},{3,8},{4,9},{5,10},{6,11},{7,12},{8,13},{9,14},{... | collective-permute-start | bytes 196616 | tf_op jit(solution)/shard_map/ppermute | solution.py:19
  62.9 22.9 %collective-permute-start.11 = (bf16[256,1,128]{0,2,1:T(8,128)(2,1)}, bf16[256,1,128]{0,2,1:T(8,128)(2,1)S(1)}, u32[]{:S(2)}, u32[]{:S(2)}) collective-permute-start(bf16[256,1,128]{0,2,1:T(8,128)(2,1)} %get-tuple-element.584), channel_id=1, source_target_pairs={{0,4},{1,5},{2,6},{3,7},{4,8},{5,9},{6,10},{7,11},{8,12},{9,13},{1... | collective-permute-start | bytes 196616 | tf_op jit(solution)/shard_map/ppermute | solution.py:19
  75.9 9.9 %collective-permute-start.12 = (bf16[256,1,128]{0,2,1:T(8,128)(2,1)}, bf16[256,1,128]{0,2,1:T(8,128)(2,1)S(1)}, u32[]{:S(2)}, u32[]{:S(2)}) collective-permute-start(bf16[256,1,128]{0,2,1:T(8,128)(2,1)} %get-tuple-element.583), channel_id=1, source_target_pairs={{0,3},{1,4},{2,5},{3,6},{4,7},{5,8},{6,9},{7,10},{8,11},{9,12},{10... | collective-permute-start | bytes 196616 | tf_op jit(solution)/shard_map/ppermute | solution.py:19
  82.1 3.7 %collective-permute-start.13 = (bf16[256,1,128]{0,2,1:T(8,128)(2,1)}, bf16[256,1,128]{0,2,1:T(8,128)(2,1)S(1)}, u32[]{:S(2)}, u32[]{:S(2)}) collective-permute-start(bf16[256,1,128]{0,2,1:T(8,128)(2,1)} %get-tuple-element.582), channel_id=1, source_target_pairs={{0,2},{1,3},{2,4},{3,5},{4,6},{5,7},{6,8},{7,9},{8,10},{9,11},{10,... | collective-permute-start | bytes 196616 | tf_op jit(solution)/shard_map/ppermute | solution.py:19
  84.0 3.6 %collective-permute-start.14 = (bf16[256,1,128]{0,2,1:T(8,128)(2,1)}, bf16[256,1,128]{0,2,1:T(8,128)(2,1)S(1)}, u32[]{:S(2)}, u32[]{:S(2)}) collective-permute-start(bf16[256,1,128]{0,2,1:T(8,128)(2,1)} %get-tuple-element.581), channel_id=1, source_target_pairs={{0,1},{1,2},{2,3},{3,4},{4,5},{5,6},{6,7},{7,8},{8,9},{9,10},{10,1... | collective-permute-start | bytes 196616 | tf_op jit(solution)/shard_map/ppermute | solution.py:19
  93.2 17.5 %copy-start.1 = (bf16[4096,128]{1,0:T(8,128)(2,1)S(1)}, bf16[4096,128]{1,0:T(8,128)(2,1)}, u32[]{:S(2)}) copy-start(bf16[4096,128]{1,0:T(8,128)(2,1)} %get-tuple-element.891) | copy-start | bytes 3145732 | tf_op jit(solution)/shard_map/while
  116.3 17.5 %copy-start.1 = (bf16[4096,128]{1,0:T(8,128)(2,1)S(1)}, bf16[4096,128]{1,0:T(8,128)(2,1)}, u32[]{:S(2)}) copy-start(bf16[4096,128]{1,0:T(8,128)(2,1)} %get-tuple-element.891) | copy-start | bytes 3145732 | tf_op jit(solution)/shard_map/while
  139.3 17.5 %copy-start.1 = (bf16[4096,128]{1,0:T(8,128)(2,1)S(1)}, bf16[4096,128]{1,0:T(8,128)(2,1)}, u32[]{:S(2)}) copy-start(bf16[4096,128]{1,0:T(8,128)(2,1)} %get-tuple-element.891) | copy-start | bytes 3145732 | tf_op jit(solution)/shard_map/while
  162.4 17.5 %copy-start.1 = (bf16[4096,128]{1,0:T(8,128)(2,1)S(1)}, bf16[4096,128]{1,0:T(8,128)(2,1)}, u32[]{:S(2)}) copy-start(bf16[4096,128]{1,0:T(8,128)(2,1)} %get-tuple-element.891) | copy-start | bytes 3145732 | tf_op jit(solution)/shard_map/while
  179.9 1.6 copy-start
  185.4 17.5 %copy-start.1 = (bf16[4096,128]{1,0:T(8,128)(2,1)S(1)}, bf16[4096,128]{1,0:T(8,128)(2,1)}, u32[]{:S(2)}) copy-start(bf16[4096,128]{1,0:T(8,128)(2,1)} %get-tuple-element.891) | copy-start | bytes 3145732 | tf_op jit(solution)/shard_map/while
  208.4 17.5 %copy-start.1 = (bf16[4096,128]{1,0:T(8,128)(2,1)S(1)}, bf16[4096,128]{1,0:T(8,128)(2,1)}, u32[]{:S(2)}) copy-start(bf16[4096,128]{1,0:T(8,128)(2,1)} %get-tuple-element.891) | copy-start | bytes 3145732 | tf_op jit(solution)/shard_map/while
  226.0 1.6 copy-start
  231.5 17.5 %copy-start.1 = (bf16[4096,128]{1,0:T(8,128)(2,1)S(1)}, bf16[4096,128]{1,0:T(8,128)(2,1)}, u32[]{:S(2)}) copy-start(bf16[4096,128]{1,0:T(8,128)(2,1)} %get-tuple-element.891) | copy-start | bytes 3145732 | tf_op jit(solution)/shard_map/while
  254.5 17.5 %copy-start.1 = (bf16[4096,128]{1,0:T(8,128)(2,1)S(1)}, bf16[4096,128]{1,0:T(8,128)(2,1)}, u32[]{:S(2)}) copy-start(bf16[4096,128]{1,0:T(8,128)(2,1)} %get-tuple-element.891) | copy-start | bytes 3145732 | tf_op jit(solution)/shard_map/while
  (6 other events, 9.6 us)
